TPU v7x, 32 devices: a whole 2x2x4 slice. The times are simulated.
32 devices in a mesh: groups: 2 (over y), seq: 4 (over z), mp: 2 (over x), enc: 2 (over core).
Axes of the slice: x: 2, y: 2, z: 4, core: 2. Of those that a mesh axis runs over, the one named last changes fastest.
Arguments:
- tokens: bfloat16 [4096, 4096], P(('groups', 'seq'), ('mp', 'enc')), parts along dimension 0, may hold values from -6 to 6
- nbr_feats: bfloat16 [192, 128, 4096], P(('groups', 'seq'), None, ('mp', 'enc')), parts along dimension 0, may hold values from -6 to 6
- counts: int32 [8], P('groups'), parts along dimension 0, may hold values from 8 to 24, as said below
- slot_target: int32 [192], P(('groups', 'seq')), parts along dimension 0, may hold values from 0 to 63, as said below
- w_query: bfloat16 [4096, 512], P(None, ('mp', 'enc')), may hold values from -32 to 32
- w_keyval: bfloat16 [4096, 512], P(None, ('mp', 'enc')), may hold values from -1 to 1
Outputs:
- attended: bfloat16 [4096, 512], P(('groups', 'seq'), ('mp', 'enc')), parts along dimension 0
There are 2 independent parts, one for each index of `groups`. A program takes and returns all parts, laid end to end along the dimension named above; an argument that names none is the same for every part. Nothing has to cross between parts.
Inputs may be any that keep to these rules, and one draw needn't show every extreme that they name: Each seq index's live slots are its first counts slots; the counts sum to 64. `slot_target`: A live slot holds neighbour o * 16 + l of the spans of seq index o; every neighbour is held by exactly one live slot; the live slots of one seq index hold at most 8 neighbours of any one seq index; dead slots hold arbitrary values of the range.
All inputs are finite; a program needn't handle non-finite values.
Results may differ from a plain program's by a relative error of at most 0.003.
The roundings to bfloat16 on the way count: a program that leaves them out, or rounds other values in their place, can miss the bound.
Values may be sent and summed in bfloat16 or wider, within the bound.
A program may use at most 128 MiB of HBM per device.

v0:
```python
import jax
import jax.numpy as jnp
from jax import lax
from jax.sharding import PartitionSpec as P

D = 4096
SPAN = 64
NBR = 2
RLEN = 128
CH_SEQ = 8
NB_SEQ = 16
ENC_CAP = 24
epsilon = 1e-05


def partner_2(block, axis, stride):
    count = lax.axis_size(axis)
    route = []
    for low in range(count):
        high = low | 1 << stride
        if high != low and high < count:
            route += [(low, high), (high, low)]
    return lax.ppermute(block, axis, route)


def passed_along(block, axis, distance):
    devices = range(lax.axis_size(axis))
    route = [(i - distance, i) for i in devices if i - distance in devices]
    return lax.ppermute(block, axis, route)


def project_fold(weight, piece):
    width = piece.shape[-1]
    flat_rows = piece.reshape(-1, width)
    mine = lax.all_to_all(weight, ("mp", "enc"), split_axis=0, concat_axis=1, tiled=True)
    partial = jnp.dot(flat_rows, mine, preferred_element_type=jnp.float32)
    running = lax.psum_scatter(partial, ("mp", "enc"), scatter_dimension=1, tiled=True)
    widened = flat_rows.astype(jnp.float32)
    squares = lax.psum(jnp.sum(widened * widened, axis=1), ("mp", "enc"))
    return (running, squares)


def normalized(carry, factor):
    running, squares = carry
    scale_rows = lax.rsqrt(squares / D + epsilon) * factor
    return (running * scale_rows[:, None]).astype(jnp.bfloat16)


def routing_plan(slot_target, counts, pair_cap):
    seq_count = counts.shape[0]
    seq_here = lax.axis_index("seq")
    live_count = jnp.sum(jnp.where(jnp.arange(seq_count) == seq_here, counts, 0))
    slot_ids = jnp.arange(ENC_CAP)
    live_slots = slot_ids < live_count
    owner_of = slot_target // NB_SEQ
    position = slot_target % NB_SEQ
    same_owner = (
        (owner_of[:, None] == owner_of[None, :])
        & live_slots[None, :]
        & (slot_ids[None, :] < slot_ids[:, None])
    )
    rank_within = jnp.sum(same_owner.astype(jnp.int32), axis=1)
    target_slot = owner_of * pair_cap + rank_within
    buffer_ids = jnp.arange(seq_count * pair_cap)
    chosen = (buffer_ids[:, None] == target_slot[None, :]) & live_slots[None, :]
    sent_ids = jnp.sum(jnp.where(chosen, position[None, :] + 1, 0), axis=1) - 1
    return (chosen, sent_ids.reshape(seq_count, pair_cap))


def pack_rows(chosen, payload, seq_count, pair_cap):
    packed = jnp.dot(chosen.astype(jnp.bfloat16), payload, preferred_element_type=jnp.float32)
    return packed.astype(jnp.bfloat16).reshape(seq_count, pair_cap, payload.shape[1])


def place_rows(received, received_ids):
    flat_rows = received.reshape(-1, received.shape[-1])
    picker = received_ids.reshape(1, -1) == jnp.arange(NB_SEQ)[:, None]
    placed = jnp.dot(picker.astype(jnp.bfloat16), flat_rows, preferred_element_type=jnp.float32)
    return placed.astype(jnp.bfloat16)


def local(tokens, nbr_feats, counts, slot_target, w_query, w_keyval):
    seq_count = lax.axis_size("seq")
    pair_cap = max(2, 2 * NB_SEQ // seq_count)
    head_size = w_keyval.shape[1]
    chosen, sent_ids = routing_plan(slot_target, counts, pair_cap)
    folded = project_fold(w_keyval, nbr_feats)
    encoded = normalized(folded, 1.0).reshape(ENC_CAP, RLEN * head_size)
    packed = pack_rows(chosen, encoded, seq_count, pair_cap)
    received, received_ids = (
        lax.all_to_all(packed, "seq", split_axis=0, concat_axis=0, tiled=True),
        lax.all_to_all(sent_ids, "seq", split_axis=0, concat_axis=0, tiled=True),
    )
    own_half = place_rows(received, received_ids).reshape(NB_SEQ, RLEN, head_size)
    partner = partner_2(own_half, "enc", 0)
    first_lane = lax.axis_index("enc") == 0
    key_rows = jnp.where(first_lane, own_half, partner).reshape(CH_SEQ, NBR * RLEN, head_size)
    value_rows = jnp.where(first_lane, partner, own_half).reshape(CH_SEQ, NBR * RLEN, head_size)
    prior_keys, prior_values = passed_along((key_rows[-1], value_rows[-1]), "seq", 1)
    context_keys = jnp.concatenate([prior_keys[None], key_rows[:-1]], axis=0)
    context_values = jnp.concatenate([prior_values[None], value_rows[:-1]], axis=0)
    folded_tokens = project_fold(w_query, tokens)
    queries = normalized(folded_tokens, head_size ** (-0.5)).reshape(CH_SEQ, SPAN, head_size)
    scores = jnp.einsum("cqd,ckd->cqk", queries, context_keys, preferred_element_type=jnp.float32)
    weights = jax.nn.softmax(scores, axis=-1).astype(jnp.bfloat16)
    attended = jnp.einsum(
        "cqk,ckd->cqd", weights, context_values, preferred_element_type=jnp.float32
    )
    return attended.astype(jnp.bfloat16).reshape(CH_SEQ * SPAN, head_size)


def solution(mesh):
    placed = (
        P(("groups", "seq"), ("mp", "enc")),
        P(("groups", "seq"), None, ("mp", "enc")),
        P("groups"),
        P(("groups", "seq")),
        P(None, ("mp", "enc")),
        P(None, ("mp", "enc")),
    )
    return jax.shard_map(
        local,
        mesh=mesh,
        in_specs=placed,
        out_specs=P(("groups", "seq"), ("mp", "enc")),
        check_vma=False,
    )
```

profile of v0, /device:TPU:0, one launch (start us, length us, event | category | flops | bytes accessed | tf_op | source)
XLA Modules:
  0.0 157.2 jit_solution(10711013462824801652)
XLA Ops:
  6.5 0.0 reduce-scatter.5.cloned.1.call-start
  6.5 18.7 %all_to_all.49 = bf16[4,1024,128]{2,1,0:T(8,128)(2,1)S(1)} all-to-all(bf16[4,1024,128]{2,1,0:T(8,128)(2,1)} %bitcast.41), channel_id=1, replica_groups=mesh['groups'=2,'seq'=4,'mp'=2,'enc'=2] {'mp','enc'}, dimensions={0} | all-to-all | bytes 2097152 | tf_op jit(solution)/shard_map/all_to_all | solution.py:35
  25.2 0.5 copy.14
  25.7 8.2 %fusion.33 = f32[3072,512]{1,0:T(8,128)} fusion(bf16[3072,1024]{1,0:T(8,128)(2,1)} %bitcast.35, bf16[1024,512]{0,1:T(8,128)(2,1)S(1)} %bitcast.42), kind=kOutput, calls=%fused_computation.53 | convolution fusion | flops 3221225472 | bytes 13631488 | tf_op jit(solution)/shard_map/dot_general | solution.py:36
  34.0 0.0 copy-start.1
  34.0 0.0 copy-start.2
  34.0 0.0 copy-start
  34.0 0.0 reduce-scatter.5.cloned.1.call-update
  34.0 0.6 copy-done.1
  34.6 0.6 fusion.22
  35.3 0.6 iota_compare_fusion.4
  35.9 0.0 copy-done.2
  36.0 0.2 convert_reduce_fusion
  36.1 0.1 select_reduce_fusion
  36.3 0.7 sub.20
  36.9 5.6 %all-to-all-start.1 = ((s32[4,1,8]{2,1,0:T(1,128)}), s32[4,1,8]{2,1,0:T(1,128)S(1)}, u32[]{:S(2)}, u32[]{:S(2)}) async-start(s32[4,1,8]{2,1,0:T(1,128)} %bitcast.4), calls=%async_computation.2 | async-start | bytes 4096 | tf_op jit(solution)/shard_map/all_to_all | solution.py:92
  42.5 0.0 copy-done
  42.5 0.3 multiply_reduce_fusion.1
  42.8 5.6 %multiply_reduce_fusion = f32[24,128]{1,0:T(8,128)S(1)} fusion(bf16[24,128,1024]{2,1,0:T(8,128)(2,1)} %param.7), kind=kLoop, calls=%fused_computation.4 | loop fusion | flops 9434112 | bytes 6303744 | tf_op jit(solution)/shard_map/reduce_sum | solution.py:39
  48.4 10.1 %all-reduce = (f32[3072]{0:T(1024)S(1)}, f32[512]{0:T(512)S(1)}) all-reduce(f32[3072]{0:T(1024)S(1)} %bitcast.51, f32[512]{0:T(512)S(1)} %multiply_reduce_fusion.1), channel_id=1, replica_groups=mesh['groups'=2,'seq'=4,'mp'=2,'enc'=2] {'mp','enc'}, use_global_device_ids=true, to_apply=%region_8.9 | all-reduce | flops 3584 | bytes 28672 | tf_op jit(solution)/shard_map/psum | solution.py:39
  58.5 0.0 all-to-all-done.1
  58.5 3.5 %all-to-all-start = ((bf16[4,1024,128]{2,1,0:T(8,128)(2,1)}), bf16[4,1024,128]{2,1,0:T(8,128)(2,1)S(1)}, u32[]{:S(2)}, u32[]{:S(2)}) async-start(bf16[4,1024,128]{2,1,0:T(8,128)(2,1)} %bitcast), calls=%async_computation | async-start | bytes 2097152 | tf_op jit(solution)/shard_map/all_to_all | solution.py:35
  62.1 42.8 %reduce-scatter.5.cloned.1.call-done = f32[3072,128]{1,0:T(8,128)} async-done(((f32[3072,512]{1,0:T(8,128)}), f32[3072,128]{1,0:T(8,128)}) %reduce-scatter.5.cloned.1.call-update) | async-done | bytes 1572880 | tf_op jit(solution)/shard_map/reduce_scatter | solution.py:37
  104.8 1.9 %multiply_convert_fusion = bf16[3072,128]{1,0:T(8,128)(2,1)S(1)} fusion(f32[3072,128]{1,0:T(8,128)} %reduce-scatter.5.cloned.1.call-done, f32[3072]{0:T(1024)S(1)} %add_rsqrt_fusion), kind=kLoop, calls=%fused_computation.6 | loop fusion | flops 786432 | bytes 2371584 | tf_op jit(solution)/shard_map/convert_element_type | solution.py:46
  106.7 0.3 reshape.70
  107.1 1.5 fusion.1
  108.6 0.0 all-to-all-done
  108.6 4.6 %all-to-all-start.3 = ((bf16[4,8,16384]{2,1,0:T(8,128)(2,1)}), bf16[4,8,16384]{2,1,0:T(8,128)(2,1)S(1)}, u32[]{:S(2)}, u32[]{:S(2)}) async-start(bf16[4,8,16384]{2,1,0:T(8,128)(2,1)} %fusion.1), calls=%async_computation.5 | async-start | bytes 2097152 | tf_op jit(solution)/shard_map/all_to_all | solution.py:91
  113.2 0.0 reduce-scatter.3.cloned.1.call-start
  113.2 0.5 copy.12
  113.8 3.0 %fusion.32 = f32[512,512]{1,0:T(8,128)} fusion(bf16[512,1024]{1,0:T(8,128)(2,1)} %param.6, bf16[1024,512]{0,1:T(8,128)(2,1)S(1)} %bitcast.43), kind=kOutput, calls=%fused_computation.52 | convolution fusion | flops 536870912 | bytes 3145728 | tf_op jit(solution)/shard_map/dot_general | solution.py:36
  116.8 0.0 reduce-scatter.3.cloned.1.call-update
  116.8 0.5 broadcast.71
  117.3 0.7 reduce.4
  118.0 0.1 eq.61
  118.1 20.9 %all-to-all-done.3 = bf16[4,8,16384]{2,1,0:T(8,128)(2,1)S(1)} async-done(((bf16[4,8,16384]{2,1,0:T(8,128)(2,1)}), bf16[4,8,16384]{2,1,0:T(8,128)(2,1)S(1)}, u32[]{:S(2)}, u32[]{:S(2)}) %all-to-all-start.3) | async-done | bytes 1048608 | tf_op jit(solution)/shard_map/all_to_all | solution.py:91
  139.0 0.3 fusion.3
  139.2 0.1 copy.15
  139.3 0.1 collective-permute-start
  139.4 1.9 %collective-permute-done = bf16[16,128,128]{2,1,0:T(8,128)(2,1)S(1)} collective-permute-done((bf16[16,128,128]{2,1,0:T(8,128)(2,1)S(1)}, bf16[16,128,128]{2,1,0:T(8,128)(2,1)S(1)}, u32[]{:S(2)}, u32[]{:S(2)}) %collective-permute-start) | collective-permute-done | bytes 524320 | tf_op jit(solution)/shard_map/ppermute | solution.py:23
  141.3 0.1 broadcast_select_fusion.1
  141.4 1.3 collective-permute-start.1
  142.7 0.0 reduce-scatter.3.cloned.1.call-done
  142.8 1.1 multiply_convert_fusion.1
  143.9 2.9 %collective-permute-start.2 = (bf16[256,128]{1,0:T(8,128)(2,1)S(1)}, bf16[256,128]{1,0:T(8,128)(2,1)S(1)}, u32[]{:S(2)}, u32[]{:S(2)}) collective-permute-start(bf16[256,128]{1,0:T(8,128)(2,1)S(1)} %bitcast.50), channel_id=1, source_target_pairs={{0,4},{4,8},{8,12},{1,5},{5,9},{9,13},{2,6},{6,10},{10,14},{3,7},{... | collective-permute-start | bytes 196616 | tf_op jit(solution)/shard_map/ppermute | solution.py:29
  146.9 0.0 collective-permute-done.1
  146.9 0.3 fusion.6
  147.2 0.5 fusion.29
  147.6 1.1 collective-permute-done.2
  148.7 1.6 %convolution_convert_fusion.2 = bf16[8,64,128]{2,1,0:T(8,128)(2,1)} fusion(bf16[7,256,128]{2,1,0:T(8,128)(2,1)S(1)} %bitcast.46, bf16[1,256,128]{2,1,0:T(8,128)(2,1)S(1)} %bitcast.52, f32[8,64]{1,0:T(8,128)S(1)} %fusion.29, f32[8,64,256]{2,1,0:T(8,128)S(1)} %fusion.6), kind=kOutput, calls=%fused_computation.10 | convolution fusion | flops 34276096 | bytes 1181696 | tf_op jit(solution)/shard_map/cqk,ckd->cqd/dot_general | solution.py:106
  (9 shorter events, 0.1 us)
Async XLA Ops:
  6.5 98.3 %reduce-scatter.5.cloned.1.call-start = ((), (), s32[]{:S(2)}) async-start(), calls=%async_computation.7 | async-start | bytes 7864320 | tf_op jit(solution)/shard_map/reduce_scatter | solution.py:37
  34.0 0.7 copy-start.1
  34.0 1.9 %copy-start.2 = (s32[24]{0:T(128)S(1)}, s32[24]{0:T(128)}, u32[]{:S(2)}) copy-start(s32[24]{0:T(128)} %param.9) | copy-start | bytes 292
  34.0 8.5 %copy-start = (bf16[512,1024]{1,0:T(8,128)(2,1)S(1)}, bf16[512,1024]{1,0:T(8,128)(2,1)}, u32[]{:S(2)}) copy-start(bf16[512,1024]{1,0:T(8,128)(2,1)} %param.6) | copy-start | bytes 3145732
  36.9 21.6 %all-to-all-start.1 = ((s32[4,1,8]{2,1,0:T(1,128)}), s32[4,1,8]{2,1,0:T(1,128)S(1)}, u32[]{:S(2)}, u32[]{:S(2)}) async-start(s32[4,1,8]{2,1,0:T(1,128)} %bitcast.4), calls=%async_computation.2 | async-start | bytes 4096 | tf_op jit(solution)/shard_map/all_to_all | solution.py:92
  58.5 50.1 %all-to-all-start = ((bf16[4,1024,128]{2,1,0:T(8,128)(2,1)}), bf16[4,1024,128]{2,1,0:T(8,128)(2,1)S(1)}, u32[]{:S(2)}, u32[]{:S(2)}) async-start(bf16[4,1024,128]{2,1,0:T(8,128)(2,1)} %bitcast), calls=%async_computation | async-start | bytes 2097152 | tf_op jit(solution)/shard_map/all_to_all | solution.py:35
  108.6 30.3 %all-to-all-start.3 = ((bf16[4,8,16384]{2,1,0:T(8,128)(2,1)}), bf16[4,8,16384]{2,1,0:T(8,128)(2,1)S(1)}, u32[]{:S(2)}, u32[]{:S(2)}) async-start(bf16[4,8,16384]{2,1,0:T(8,128)(2,1)} %fusion.1), calls=%async_computation.5 | async-start | bytes 2097152 | tf_op jit(solution)/shard_map/all_to_all | solution.py:91
  113.2 29.5 %reduce-scatter.3.cloned.1.call-start = ((), (), s32[]{:S(2)}) async-start(), calls=%async_computation.6 | async-start | bytes 1310720 | tf_op jit(solution)/shard_map/reduce_scatter | solution.py:37
  139.3 2.0 %collective-permute-start = (bf16[16,128,128]{2,1,0:T(8,128)(2,1)S(1)}, bf16[16,128,128]{2,1,0:T(8,128)(2,1)S(1)}, u32[]{:S(2)}, u32[]{:S(2)}) collective-permute-start(bf16[16,128,128]{2,1,0:T(8,128)(2,1)S(1)} %bitcast.38), channel_id=1, source_target_pairs={{0,1},{1,0},{2,3},{3,2},{4,5},{5,4},{6,7},{7,6},{8,9},{9,8},{10,11... | collective-permute-start | bytes 1572872 | tf_op jit(solution)/shard_map/ppermute | solution.py:23
  141.4 5.4 %collective-permute-start.1 = (bf16[256,128]{1,0:T(8,128)(2,1)S(1)}, bf16[256,128]{1,0:T(8,128)(2,1)S(1)}, u32[]{:S(2)}, u32[]{:S(2)}) collective-permute-start(bf16[256,128]{1,0:T(8,128)(2,1)S(1)} %bitcast.49), channel_id=1, source_target_pairs={{0,4},{4,8},{8,12},{1,5},{5,9},{9,13},{2,6},{6,10},{10,14},{3,7},{... | collective-permute-start | bytes 196616 | tf_op jit(solution)/shard_map/ppermute | solution.py:29
  143.9 4.8 %collective-permute-start.2 = (bf16[256,128]{1,0:T(8,128)(2,1)S(1)}, bf16[256,128]{1,0:T(8,128)(2,1)S(1)}, u32[]{:S(2)}, u32[]{:S(2)}) collective-permute-start(bf16[256,128]{1,0:T(8,128)(2,1)S(1)} %bitcast.50), channel_id=1, source_target_pairs={{0,4},{4,8},{8,12},{1,5},{5,9},{9,13},{2,6},{6,10},{10,14},{3,7},{... | collective-permute-start | bytes 196616 | tf_op jit(solution)/shard_map/ppermute | solution.py:29
Sparse Core Ops, SparseCore 0:
  34.1 70.6 reduce-scatter.4
  116.9 25.3 reduce-scatter.2
where the time goes:
time: 158 us; the launch traced here: 157 us
  waiting for transfers between devices  66.7 us (42%)
  blocking collectives  28.8 us (18%)
  starting transfers between devices  18 us (11%)
  matrix products  15.4 us (10%)
  between operations  13.6 us (9%)
  other arithmetic  11.2 us (7%)
  local copies, waits for them, and re-layouts  3.44 us (2%)
    reduce_scatter x2, waiting for transfers between devices, project_fold(): lax.psum_scatter(partial, ('mp', 'enc'), scatter_dimension=1, tiled=True)  42.8 us
    all_to_all x1, waiting for transfers between devices, local(): lax.all_to_all(packed, 'seq', split_axis=0, concat_axis=0, tiled=True)  20.9 us
    all_to_all x1, blocking collectives, project_fold(): lax.all_to_all(weight, ('mp', 'enc'), split_axis=0, concat_axis=1, tiled=...  18.7 us
    dot_general x2, matrix products, project_fold(): partial = jnp.dot(flat_rows, mine, preferred_element_type=jnp.float32)  11.3 us
    psum x1, blocking collectives, project_fold(): squares = lax.psum(jnp.sum(widened * widened, axis=1), ('mp', 'enc'))  10.1 us
    reduce_sum x2, other arithmetic, project_fold(): squares = lax.psum(jnp.sum(widened * widened, axis=1), ('mp', 'enc'))  5.83 us
    all_to_all x1, starting transfers between devices, local(): lax.all_to_all(sent_ids, 'seq', split_axis=0, concat_axis=0, tiled=True)  5.6 us
    all_to_all x1, starting transfers between devices, local(): lax.all_to_all(packed, 'seq', split_axis=0, concat_axis=0, tiled=True)  4.63 us
  transfers between devices with their start and end apart: 8, of which 4 were waited for; matrix products, arithmetic and copies ran while one was open for 12% of the time, Pallas kernels for 0%

commit v1 on v0

--- a/solution.py
+++ b/solution.py
@@ -11,6 +11,29 @@
 NB_SEQ = 16
 ENC_CAP = 24
 epsilon = 1e-05
+
+
+def in_blocks(value, dim, count):
+    shape = value.shape
+    blocks = value.reshape(*shape[:dim], count, shape[dim] // count, *shape[dim + 1 :])
+    return jnp.moveaxis(blocks, dim, 0)
+
+
+def laid_out(parts, dim):
+    shape = list(parts.shape[1:])
+    shape[dim] *= parts.shape[0]
+    return jnp.moveaxis(parts, 0, dim).reshape(shape)
+
+
+def rotated_exchange(x, axis, split_dim, concat_dim):
+    length, index = (lax.axis_size(axis), lax.axis_index(axis))
+    pieces = in_blocks(x, split_dim, length)
+    outs = [pieces[index]]
+    for hop in range(1, length):
+        sent = pieces[(index + hop) % length]
+        outs.append(lax.ppermute(sent, axis, [(i, (i + hop) % length) for i in range(length)]))
+    pieces = jnp.stack(outs)[(index - jnp.arange(length)) % length]
+    return laid_out(pieces, concat_dim)
 
 
 def partner_2(block, axis, stride):
@@ -89,7 +112,7 @@
     packed = pack_rows(chosen, encoded, seq_count, pair_cap)
     received, received_ids = (
         lax.all_to_all(packed, "seq", split_axis=0, concat_axis=0, tiled=True),
-        lax.all_to_all(sent_ids, "seq", split_axis=0, concat_axis=0, tiled=True),
+        rotated_exchange(sent_ids, "seq", 0, 0),
     )
     own_half = place_rows(received, received_ids).reshape(NB_SEQ, RLEN, head_size)
     partner = partner_2(own_half, "enc", 0)

time: 158 us -> 148 us (0.937)
  waiting for transfers between devices: 66.7 us -> 54.2 us
  blocking collectives: 28.8 us -> 34.2 us
  other arithmetic: 11.2 us -> 9.31 us
    all_to_all x1, waiting for transfers between devices: 20.9 us -> 0.01 us  [local(): lax.all_to_all(packed, 'seq', split_axis=0, concat_axis=0, tiled=True)]
    ppermute x0 -> x3, waiting for transfers between devices: none -> 17 us  [rotated_exchange(): lax.ppermute(sent, axis, [(i, (i + hop) % length) for i in range(length)])]
    reduce_scatter x2, waiting for transfers between devices: 42.8 us -> 34.2 us  [project_fold(): lax.psum_scatter(partial, ('mp', 'enc'), scatter_dimension=1, tiled=True)]
    all_to_all x1 -> x0, starting transfers between devices: 5.6 us -> none  [local(): lax.all_to_all(sent_ids, 'seq', split_axis=0, concat_axis=0, tiled=True)]
    psum x1, blocking collectives: 10.1 us -> 15.5 us  [project_fold(): squares = lax.psum(jnp.sum(widened * widened, axis=1), ('mp', 'enc'))]
    ppermute x0 -> x3, starting transfers between devices: none -> 5 us  [rotated_exchange(): lax.ppermute(sent, axis, [(i, (i + hop) % length) for i in range(length)])]
  transfers between devices with their start and end apart: 8 -> 10, of which waited for: 4 -> 5; matrix products, arithmetic and copies ran while one was open for 12% -> 11% of each run, Pallas kernels for 0% -> 0%
where the time goes in v1:
time: 148 us; the launch traced here: 147 us
  waiting for transfers between devices  54.2 us (37%)
  blocking collectives  34.2 us (23%)
  starting transfers between devices  18.2 us (12%)
  matrix products  15.5 us (10%)
  between operations  13.7 us (9%)
  other arithmetic  9.31 us (6%)
  local copies, waits for them, and re-layouts  2.31 us (2%)
    reduce_scatter x2, waiting for transfers between devices, project_fold(): lax.psum_scatter(partial, ('mp', 'enc'), scatter_dimension=1, tiled=True)  34.2 us
    all_to_all x1, blocking collectives, project_fold(): lax.all_to_all(weight, ('mp', 'enc'), split_axis=0, concat_axis=1, tiled=...  18.7 us
    ppermute x3, waiting for transfers between devices, rotated_exchange(): lax.ppermute(sent, axis, [(i, (i + hop) % length) for i in range(length)])  17 us
    psum x1, blocking collectives, project_fold(): squares = lax.psum(jnp.sum(widened * widened, axis=1), ('mp', 'enc'))  15.5 us
    dot_general x2, matrix products, project_fold(): partial = jnp.dot(flat_rows, mine, preferred_element_type=jnp.float32)  11.2 us
    ppermute x3, starting transfers between devices, rotated_exchange(): lax.ppermute(sent, axis, [(i, (i + hop) % length) for i in range(length)])  5 us
    ppermute x2, starting transfers between devices, passed_along(): return lax.ppermute(block, axis, route)  4.85 us
    all_to_all x1, starting transfers between devices, local(): lax.all_to_all(packed, 'seq', split_axis=0, concat_axis=0, tiled=True)  4.65 us
  transfers between devices with their start and end apart: 10, of which 5 were waited for; matrix products, arithmetic and copies ran while one was open for 11% of the time, Pallas kernels for 0%

profile of v1, /device:TPU:0, one launch (start us, length us, event | category | flops | bytes accessed | tf_op | source)
XLA Modules:
  0.0 147.4 jit_solution(7517138141742332268)
XLA Ops:
  6.5 0.0 reduce-scatter.5.cloned.1.call-start
  6.5 18.7 %all_to_all.43 = bf16[4,1024,128]{2,1,0:T(8,128)(2,1)S(1)} all-to-all(bf16[4,1024,128]{2,1,0:T(8,128)(2,1)} %bitcast.59), channel_id=1, replica_groups=mesh['groups'=2,'seq'=4,'mp'=2,'enc'=2] {'mp','enc'}, dimensions={0} | all-to-all | bytes 2097152 | tf_op jit(solution)/shard_map/all_to_all | solution.py:58
  25.2 0.5 copy.22
  25.7 8.2 %fusion.38 = f32[3072,512]{1,0:T(8,128)} fusion(bf16[3072,1024]{1,0:T(8,128)(2,1)} %bitcast.53, bf16[1024,512]{0,1:T(8,128)(2,1)S(1)} %bitcast.60), kind=kOutput, calls=%fused_computation.69 | convolution fusion | flops 3221225472 | bytes 13631488 | tf_op jit(solution)/shard_map/dot_general | solution.py:59
  34.0 0.0 copy-start
  34.0 0.0 reduce-scatter.5.cloned.1.call-update
  34.0 0.0 copy-start.1
  34.0 0.0 copy-start.2
  34.0 3.7 %all-to-all-start = ((bf16[4,1024,128]{2,1,0:T(8,128)(2,1)}), bf16[4,1024,128]{2,1,0:T(8,128)(2,1)S(1)}, u32[]{:S(2)}, u32[]{:S(2)}) async-start(bf16[4,1024,128]{2,1,0:T(8,128)(2,1)} %bitcast), calls=%async_computation | async-start | bytes 2097152 | tf_op jit(solution)/shard_map/all_to_all | solution.py:58
  37.7 0.0 copy-done
  37.7 0.3 multiply_reduce_fusion.1
  38.0 4.3 %multiply_reduce_fusion = f32[24,128]{1,0:T(8,128)S(1)} fusion(bf16[24,128,1024]{2,1,0:T(8,128)(2,1)} %param.7), kind=kLoop, calls=%fused_computation.5 | loop fusion | flops 9434112 | bytes 6303744 | tf_op jit(solution)/shard_map/reduce_sum | solution.py:62
  42.3 15.5 %all-reduce = (f32[3072]{0:T(1024)S(1)}, f32[512]{0:T(512)S(1)}) all-reduce(f32[3072]{0:T(1024)S(1)} %bitcast.69, f32[512]{0:T(512)S(1)} %multiply_reduce_fusion.1), channel_id=1, replica_groups=mesh['groups'=2,'seq'=4,'mp'=2,'enc'=2] {'mp','enc'}, use_global_device_ids=true, to_apply=%region_8.9 | all-reduce | flops 3584 | bytes 28672 | tf_op jit(solution)/shard_map/psum | solution.py:62
  57.9 0.0 copy-done.1
  57.9 0.6 fusion.25
  58.5 0.6 iota_compare_fusion.4
  59.2 0.0 copy-done.2
  59.2 0.2 convert_reduce_fusion
  59.4 34.2 %reduce-scatter.5.cloned.1.call-done = f32[3072,128]{1,0:T(8,128)} async-done(((f32[3072,512]{1,0:T(8,128)}), f32[3072,128]{1,0:T(8,128)}) %reduce-scatter.5.cloned.1.call-update) | async-done | bytes 1572880 | tf_op jit(solution)/shard_map/reduce_scatter | solution.py:60
  93.6 1.9 %multiply_convert_fusion = bf16[3072,128]{1,0:T(8,128)(2,1)S(1)} fusion(f32[3072,128]{1,0:T(8,128)} %reduce-scatter.5.cloned.1.call-done, f32[3072]{0:T(1024)S(1)} %add_rsqrt_fusion), kind=kLoop, calls=%fused_computation.7 | loop fusion | flops 786432 | bytes 2371584 | tf_op jit(solution)/shard_map/convert_element_type | solution.py:69
  95.4 0.3 reshape.113
  95.8 1.5 %fusion.1 = bf16[4,8,16384]{2,1,0:T(8,128)(2,1)} fusion(bf16[24,16384]{1,0:T(8,128)(2,1)S(1)} %reshape.113, s32[24]{0:T(128)S(1)} %multiply_add_fusion, pred[24]{0:T(512)(128)(4,1)S(1)} %iota_compare_fusion.4), kind=kOutput, calls=%fused_computation.3 | convolution fusion | flops 25691648 | bytes 1835128 | tf_op jit(solution)/shard_map/dot_general | solution.py:94
  97.3 0.0 all-to-all-done
  97.3 4.6 %all-to-all-start.2 = ((bf16[4,8,16384]{2,1,0:T(8,128)(2,1)}), bf16[4,8,16384]{2,1,0:T(8,128)(2,1)S(1)}, u32[]{:S(2)}, u32[]{:S(2)}) async-start(bf16[4,8,16384]{2,1,0:T(8,128)(2,1)} %fusion.1), calls=%async_computation.4 | async-start | bytes 2097152 | tf_op jit(solution)/shard_map/all_to_all | solution.py:114
  102.0 0.0 reduce-scatter.3.cloned.1.call-start
  102.0 0.5 copy.18
  102.5 3.0 %fusion.37 = f32[512,512]{1,0:T(8,128)} fusion(bf16[512,1024]{1,0:T(8,128)(2,1)} %param.6, bf16[1024,512]{0,1:T(8,128)(2,1)S(1)} %bitcast.61), kind=kOutput, calls=%fused_computation.68 | convolution fusion | flops 536870912 | bytes 3145728 | tf_op jit(solution)/shard_map/dot_general | solution.py:59
  105.5 0.0 reduce-scatter.3.cloned.1.call-update
  105.6 0.1 select_reduce_fusion
  105.7 0.1 sub.31
  105.8 3.9 %collective-permute-start.2 = (s32[1,8]{1,0:T(1,128)S(1)}, s32[1,8]{1,0:T(1,128)S(1)}, u32[]{:S(2)}, u32[]{:S(2)}) collective-permute-start(s32[1,8]{1,0:T(1,128)S(1)} %get-tuple-element.10), channel_id=1, source_target_pairs={{0,12},{4,0},{8,4},{12,8},{1,13},{5,1},{9,5},{13,9},{2,14},{6,2},{... | collective-permute-start | bytes 104 | tf_op jit(solution)/shard_map/ppermute | solution.py:34
  109.7 0.0 collective-permute-start.1
  109.7 1.1 collective-permute-start
  110.8 8.3 %collective-permute-done.2 = s32[1,8]{1,0:T(1,128)S(1)} collective-permute-done((s32[1,8]{1,0:T(1,128)S(1)}, s32[1,8]{1,0:T(1,128)S(1)}, u32[]{:S(2)}, u32[]{:S(2)}) %collective-permute-start.2) | collective-permute-done | bytes 64 | tf_op jit(solution)/shard_map/ppermute | solution.py:34
  119.1 8.6 %collective-permute-done.1 = s32[1,8]{1,0:T(1,128)S(1)} collective-permute-done((s32[1,8]{1,0:T(1,128)S(1)}, s32[1,8]{1,0:T(1,128)S(1)}, u32[]{:S(2)}, u32[]{:S(2)}) %collective-permute-start.1) | collective-permute-done | bytes 64 | tf_op jit(solution)/shard_map/ppermute | solution.py:34
  127.8 0.0 collective-permute-done
  127.8 0.6 gather_fusion
  128.4 0.1 eq.70
  128.5 0.0 all-to-all-done.2
  128.5 0.3 fusion.3
  128.8 0.1 copy.23
  128.8 0.1 collective-permute-start.3
  128.9 1.9 %collective-permute-done.3 = bf16[16,128,128]{2,1,0:T(8,128)(2,1)S(1)} collective-permute-done((bf16[16,128,128]{2,1,0:T(8,128)(2,1)S(1)}, bf16[16,128,128]{2,1,0:T(8,128)(2,1)S(1)}, u32[]{:S(2)}, u32[]{:S(2)}) %collective-permute-start.3) | collective-permute-done | bytes 524320 | tf_op jit(solution)/shard_map/ppermute | solution.py:46
  130.8 0.1 broadcast_select_fusion.1
  130.9 2.4 %collective-permute-start.4 = (bf16[256,128]{1,0:T(8,128)(2,1)S(1)}, bf16[256,128]{1,0:T(8,128)(2,1)S(1)}, u32[]{:S(2)}, u32[]{:S(2)}) collective-permute-start(bf16[256,128]{1,0:T(8,128)(2,1)S(1)} %bitcast.67), channel_id=1, source_target_pairs={{0,4},{4,8},{8,12},{1,5},{5,9},{9,13},{2,6},{6,10},{10,14},{3,7},{... | collective-permute-start | bytes 196616 | tf_op jit(solution)/shard_map/ppermute | solution.py:52
  133.3 0.0 reduce-scatter.3.cloned.1.call-done
  133.4 1.1 multiply_convert_fusion.1
  134.6 2.5 %collective-permute-start.5 = (bf16[256,128]{1,0:T(8,128)(2,1)S(1)}, bf16[256,128]{1,0:T(8,128)(2,1)S(1)}, u32[]{:S(2)}, u32[]{:S(2)}) collective-permute-start(bf16[256,128]{1,0:T(8,128)(2,1)S(1)} %bitcast.68), channel_id=1, source_target_pairs={{0,4},{4,8},{8,12},{1,5},{5,9},{9,13},{2,6},{6,10},{10,14},{3,7},{... | collective-permute-start | bytes 196616 | tf_op jit(solution)/shard_map/ppermute | solution.py:52
  137.0 0.0 collective-permute-done.4
  137.0 0.3 fusion.6
  137.3 0.5 fusion.34
  137.8 1.1 collective-permute-done.5
  138.9 1.6 %convolution_convert_fusion.2 = bf16[8,64,128]{2,1,0:T(8,128)(2,1)} fusion(bf16[7,256,128]{2,1,0:T(8,128)(2,1)S(1)} %bitcast.64, bf16[1,256,128]{2,1,0:T(8,128)(2,1)S(1)} %bitcast.73, f32[8,64]{1,0:T(8,128)S(1)} %fusion.34, f32[8,64,256]{2,1,0:T(8,128)S(1)} %fusion.6), kind=kOutput, calls=%fused_computation.11 | convolution fusion | flops 34276096 | bytes 1181696 | tf_op jit(solution)/shard_map/cqk,ckd->cqd/dot_general | solution.py:129
  (13 shorter events, 0.2 us)
Async XLA Ops:
  6.5 87.0 %reduce-scatter.5.cloned.1.call-start = ((), (), s32[]{:S(2)}) async-start(), calls=%async_computation.6 | async-start | bytes 7864320 | tf_op jit(solution)/shard_map/reduce_scatter | solution.py:60
  34.0 3.7 %copy-start = (bf16[512,1024]{1,0:T(8,128)(2,1)S(1)}, bf16[512,1024]{1,0:T(8,128)(2,1)}, u32[]{:S(2)}) copy-start(bf16[512,1024]{1,0:T(8,128)(2,1)} %param.6) | copy-start | bytes 3145732
  34.0 23.9 %copy-start.1 = (s32[4]{0:T(128)S(1)}, s32[4]{0:T(128)}, u32[]{:S(2)}) copy-start(s32[4]{0:T(128)} %param.8) | copy-start | bytes 52
  34.0 25.1 %copy-start.2 = (s32[24]{0:T(128)S(1)}, s32[24]{0:T(128)}, u32[]{:S(2)}) copy-start(s32[24]{0:T(128)} %param.9) | copy-start | bytes 292
  34.0 63.3 %all-to-all-start = ((bf16[4,1024,128]{2,1,0:T(8,128)(2,1)}), bf16[4,1024,128]{2,1,0:T(8,128)(2,1)S(1)}, u32[]{:S(2)}, u32[]{:S(2)}) async-start(bf16[4,1024,128]{2,1,0:T(8,128)(2,1)} %bitcast), calls=%async_computation | async-start | bytes 2097152 | tf_op jit(solution)/shard_map/all_to_all | solution.py:58
  97.3 31.1 %all-to-all-start.2 = ((bf16[4,8,16384]{2,1,0:T(8,128)(2,1)}), bf16[4,8,16384]{2,1,0:T(8,128)(2,1)S(1)}, u32[]{:S(2)}, u32[]{:S(2)}) async-start(bf16[4,8,16384]{2,1,0:T(8,128)(2,1)} %fusion.1), calls=%async_computation.4 | async-start | bytes 2097152 | tf_op jit(solution)/shard_map/all_to_all | solution.py:114
  102.0 31.4 %reduce-scatter.3.cloned.1.call-start = ((), (), s32[]{:S(2)}) async-start(), calls=%async_computation.5 | async-start | bytes 1310720 | tf_op jit(solution)/shard_map/reduce_scatter | solution.py:60
  105.8 13.4 %collective-permute-start.2 = (s32[1,8]{1,0:T(1,128)S(1)}, s32[1,8]{1,0:T(1,128)S(1)}, u32[]{:S(2)}, u32[]{:S(2)}) collective-permute-start(s32[1,8]{1,0:T(1,128)S(1)} %get-tuple-element.10), channel_id=1, source_target_pairs={{0,12},{4,0},{8,4},{12,8},{1,13},{5,1},{9,5},{13,9},{2,14},{6,2},{... | collective-permute-start | bytes 104 | tf_op jit(solution)/shard_map/ppermute | solution.py:34
  109.7 18.1 %collective-permute-start.1 = (s32[1,8]{1,0:T(1,128)S(1)}, s32[1,8]{1,0:T(1,128)S(1)}, u32[]{:S(2)}, u32[]{:S(2)}) collective-permute-start(s32[1,8]{1,0:T(1,128)S(1)} %get-tuple-element.11), channel_id=1, source_target_pairs={{0,8},{4,12},{8,0},{12,4},{1,9},{5,13},{9,1},{13,5},{2,10},{6,14},... | collective-permute-start | bytes 104 | tf_op jit(solution)/shard_map/ppermute | solution.py:34
  109.7 18.1 %collective-permute-start = (s32[1,8]{1,0:T(1,128)S(1)}, s32[1,8]{1,0:T(1,128)S(1)}, u32[]{:S(2)}, u32[]{:S(2)}) collective-permute-start(s32[1,8]{1,0:T(1,128)S(1)} %get-tuple-element.12), channel_id=1, source_target_pairs={{0,4},{4,8},{8,12},{12,0},{1,5},{5,9},{9,13},{13,1},{2,6},{6,10},{... | collective-permute-start | bytes 104 | tf_op jit(solution)/shard_map/ppermute | solution.py:34
  128.8 2.0 %collective-permute-start.3 = (bf16[16,128,128]{2,1,0:T(8,128)(2,1)S(1)}, bf16[16,128,128]{2,1,0:T(8,128)(2,1)S(1)}, u32[]{:S(2)}, u32[]{:S(2)}) collective-permute-start(bf16[16,128,128]{2,1,0:T(8,128)(2,1)S(1)} %bitcast.56), channel_id=1, source_target_pairs={{0,1},{1,0},{2,3},{3,2},{4,5},{5,4},{6,7},{7,6},{8,9},{9,8},{10,11... | collective-permute-start | bytes 1572872 | tf_op jit(solution)/shard_map/ppermute | solution.py:46
  130.9 6.1 %collective-permute-start.4 = (bf16[256,128]{1,0:T(8,128)(2,1)S(1)}, bf16[256,128]{1,0:T(8,128)(2,1)S(1)}, u32[]{:S(2)}, u32[]{:S(2)}) collective-permute-start(bf16[256,128]{1,0:T(8,128)(2,1)S(1)} %bitcast.67), channel_id=1, source_target_pairs={{0,4},{4,8},{8,12},{1,5},{5,9},{9,13},{2,6},{6,10},{10,14},{3,7},{... | collective-permute-start | bytes 196616 | tf_op jit(solution)/shard_map/ppermute | solution.py:52
  134.6 4.4 %collective-permute-start.5 = (bf16[256,128]{1,0:T(8,128)(2,1)S(1)}, bf16[256,128]{1,0:T(8,128)(2,1)S(1)}, u32[]{:S(2)}, u32[]{:S(2)}) collective-permute-start(bf16[256,128]{1,0:T(8,128)(2,1)S(1)} %bitcast.68), channel_id=1, source_target_pairs={{0,4},{4,8},{8,12},{1,5},{5,9},{9,13},{2,6},{6,10},{10,14},{3,7},{... | collective-permute-start | bytes 196616 | tf_op jit(solution)/shard_map/ppermute | solution.py:52
Sparse Core Ops, SparseCore 0:
  34.1 59.3 reduce-scatter.4
  105.7 25.3 reduce-scatter.2
